TPU v7x, 128 devices: a whole 4x4x4 slice. The times are simulated.
128 devices in a mesh: row: 16 (over y, x), col: 8 (over z, core).
Axes of the slice: x: 4, y: 4, z: 4, core: 2. Of those that a mesh axis runs over, the one named last changes fastest.
Arguments:
- features: float32 [32768, 256], P(('row', 'col')), may hold values from -6 to 6
- loader_perm: int32 [32768], P(('row', 'col')), may hold values from 0 to 32767, as said below
- block_values: float32 [16, 8, 256, 4096], P('row', 'col'), may hold values from -0.09375 to 0.09375
- block_row: int32 [16, 8, 256], P('row', 'col'), may hold values from 0 to 63
- block_column: int32 [16, 8, 256], P('row', 'col'), may hold values from 0 to 31
- tile_count: int32 [16, 8], P('row', 'col'), may hold values from 32 to 256, as said below
- weight: float32 [256, 256], replicated, may hold values from -0.375 to 0.375
- bias_vector: float32 [256], replicated, may hold values from -0.5 to 0.5
- cotangent: float32 [32768, 256], P(('row', 'col')), may hold values from -6 to 6
Outputs:
- output: float32 [32768, 256], P(('row', 'col'))
- grad_x: float32 [32768, 256], P(('row', 'col'))
- grad_w: float32 [256, 256], replicated
- grad_b: float32 [256], replicated
Inputs may be any that keep to these rules, and one draw needn't show every extreme that they name: `loader_perm`: every grid position appears once; the 256 loader rows of any one device name the same number of positions, 256 divided by the number of devices, in each aligned block of 256 grid positions. `tile_count`: every count is 256 divided by 1, 2, 4 or 8; a block position may appear in several slots of a tile, and such blocks add.
All inputs are finite; a program needn't handle non-finite values.
Results may differ from a plain program's by a relative error of at most 0.0003.
Values sent between devices are 32-bit elements; how exact they have to be, the bound alone decides.
No kernel may reach another device: no remote copies, remote signals or barrier semaphores. Data moves between devices by JAX's collectives and lax.ppermute only.
A program may use at most 128 MiB of HBM per device.

v0:
```python
import math
import jax
import jax.numpy as jnp
from jax import lax
from jax.sharding import PartitionSpec as P

precise = lax.Precision.HIGHEST


def accumulate(
    accumulated,
    source_blocks,
    tile_vals,
    source_at,
    target_at,
    live_count,
    pattern,
    group_size,
    group_turns,
    block_size,
):

    def one_group(turn, partial_sum):
        first_slot = turn * group_size
        group_vals = lax.dynamic_slice_in_dim(tile_vals, first_slot, group_size, 0)
        from_at = lax.dynamic_slice_in_dim(source_at, first_slot, group_size, 0)
        into_at = lax.dynamic_slice_in_dim(target_at, first_slot, group_size, 0)
        alive = first_slot + jnp.arange(group_size, dtype=jnp.int32) < live_count
        group_vals = jnp.where(alive[:, None], group_vals, jnp.zeros_like(group_vals))
        group_vals = group_vals.reshape(group_size, block_size, block_size)
        terms = jnp.einsum(pattern, group_vals, source_blocks[from_at], precision=precise)
        return partial_sum.at[into_at].add(terms)

    return lax.fori_loop(0, group_turns, one_group, accumulated)


def on_device(
    features,
    loader_perm,
    block_values,
    block_row,
    block_column,
    tile_count,
    weight,
    bias_vector,
    cotangent,
):
    node_dev, feat_width = features.shape
    row_devices = lax.axis_size("row")
    col_devices = lax.axis_size("col")
    devices = row_devices * col_devices
    row_index = lax.axis_index("row")
    group_rows = col_devices * node_dev
    tile_vals = block_values[0, 0]
    tile_rows = block_row[0, 0]
    tile_columns = block_column[0, 0]
    live_count = tile_count[0, 0]
    block_size = math.isqrt(tile_vals.shape[-1])
    slot_total = tile_vals.shape[0]
    group_size = math.gcd(slot_total, 128)
    group_turns = slot_total // group_size
    per_group = node_dev // row_devices
    ordering = jnp.argsort(loader_perm // group_rows, stable=True)
    sent_rows = jnp.broadcast_to(
        features[ordering].reshape(row_devices, 1, per_group, feat_width),
        (row_devices, col_devices, per_group, feat_width),
    ).reshape(devices, per_group, feat_width)
    sent_ids = jnp.broadcast_to(
        loader_perm[ordering].astype(jnp.float32).reshape(row_devices, 1, per_group),
        (row_devices, col_devices, per_group),
    ).reshape(devices, per_group)
    got_rows, got_ids = (
        lax.all_to_all(sent_rows, ("row", "col"), split_axis=0, concat_axis=0, tiled=True),
        lax.all_to_all(sent_ids, ("row", "col"), split_axis=0, concat_axis=0, tiled=True),
    )
    local_pos = got_ids.reshape(group_rows).astype(jnp.int32) - row_index * group_rows
    panel_rows = got_rows.reshape(group_rows, feat_width)[jnp.argsort(local_pos)]
    out_blocks = row_devices * node_dev // block_size
    in_blocks = group_rows // block_size
    partial_value = accumulate(
        jnp.zeros((out_blocks, block_size, feat_width), jnp.float32),
        panel_rows.reshape(in_blocks, block_size, feat_width),
        tile_vals,
        tile_columns,
        tile_rows,
        live_count,
        "kab,kbf->kaf",
        group_size,
        group_turns,
        block_size,
    )
    partial_value = partial_value.reshape(row_devices * node_dev, feat_width)
    hidden = lax.psum_scatter(partial_value, "row", scatter_dimension=0, tiled=True)
    preact = jnp.dot(hidden, weight, precision=precise) + bias_vector
    squashed = jax.nn.sigmoid(preact)
    output = preact * squashed
    grad_pre = cotangent * squashed * (1.0 + preact * (1.0 - squashed))
    grad_hidden = jnp.dot(grad_pre, weight.T, precision=precise)
    column = lax.all_gather(grad_hidden, "row", axis=0, tiled=True)
    partial_x = accumulate(
        jnp.zeros((in_blocks, block_size, feat_width), jnp.float32),
        column.reshape(out_blocks, block_size, feat_width),
        tile_vals,
        tile_rows,
        tile_columns,
        live_count,
        "kba,kbf->kaf",
        group_size,
        group_turns,
        block_size,
    )
    grad_x = lax.psum_scatter(
        partial_x.reshape(group_rows, feat_width), "col", scatter_dimension=0, tiled=True
    )
    local_w = jnp.einsum("nf,ng->fg", hidden, grad_pre, precision=precise)
    local_b = jnp.sum(grad_pre, axis=0)
    grad_w, grad_b = lax.psum((local_w, local_b), ("row", "col"))
    norm_scale = 1.0 / math.sqrt(node_dev * devices)
    return (output, grad_x, grad_w * norm_scale, grad_b * norm_scale)


def solution(mesh):
    in_specs = (
        P(("row", "col"), None),
        P(("row", "col")),
        P("row", "col", None, None),
        P("row", "col", None),
        P("row", "col", None),
        P("row", "col"),
        P(),
        P(),
        P(("row", "col"), None),
    )
    out_specs = (P(("row", "col"), None), P(("row", "col"), None), P(), P())
    return jax.shard_map(
        on_device, mesh=mesh, in_specs=in_specs, out_specs=out_specs, check_vma=False
    )
```

profile of v0, /device:TPU:0, one launch (start us, length us, event | category | flops | bytes accessed | tf_op | source)
XLA Modules:
  0.0 511.8 jit_solution(5584946851250367723)
XLA Ops:
  7.2 0.7 and_select_fusion
  7.9 3.2 sort.34
  11.1 2.0 gather_fusion.3
  13.8 11.2 %all-to-all-start.1 = ((f32[128,1,16]{2,1,0:T(1,128)}), f32[128,1,16]{2,1,0:T(1,128)S(1)}, u32[]{:S(2)}, u32[]{:S(2)}) async-start(f32[128,1,16]{2,1,0:T(1,128)} %bitcast.9), calls=%async_computation.1 | async-start | bytes 131072 | tf_op jit(solution)/shard_map/all_to_all | solution.py:74
  25.0 1.9 gather_fusion.2
  26.9 7.5 %all-to-all-done.1 = f32[128,1,16]{2,1,0:T(1,128)S(1)} async-done(((f32[128,1,16]{2,1,0:T(1,128)}), f32[128,1,16]{2,1,0:T(1,128)S(1)}, u32[]{:S(2)}, u32[]{:S(2)}) %all-to-all-start.1) | async-done | bytes 8224 | tf_op jit(solution)/shard_map/all_to_all | solution.py:74
  34.5 1.6 broadcast_in_dim.96
  36.1 4.6 all-to-all-start
  40.8 5.6 %copy.19 = f32[1,1,256,4096]{2,3,1,0:T(8,128)} copy(f32[1,1,256,4096]{3,2,1,0:T(8,128)} %param.15) | data formatting | bytes 8388608 | tf_op args[2]
  46.7 5.0 sort.35
  51.7 19.4 %all-to-all-done = f32[128,16,256]{2,1,0:T(8,128)S(1)} async-done(((f32[128,16,256]{2,1,0:T(8,128)}), f32[128,16,256]{2,1,0:T(8,128)S(1)}, u32[]{:S(2)}, u32[]{:S(2)}) %all-to-all-start) | async-done | bytes 2097184 | tf_op jit(solution)/shard_map/all_to_all | solution.py:73
  71.1 1.3 copy-done.3
  72.5 8.2 %gather_fusion.4 = f32[2048,256]{1,0:T(8,128)S(1)} fusion(f32[2048,256]{1,0:T(8,128)} %bitcast.42, s32[2048]{0:T(1024)S(1)} %fusion.1), kind=kCustom, calls=%fused_computation.4 | custom fusion | bytes 4202496 | tf_op jit(solution)/shard_map/gather | solution.py:77
  80.8 2.5 broadcast_in_dim.93
  83.2 111.6 %while.26 = (s32[]{:T(128)}, f32[64,64,256]{2,1,0:T(8,128)}, s32[256]{0:T(256)S(1)}, s32[]{:T(128)}, f32[256,4096]{0,1:T(8,128)}, /*index=5*/s32[256]{0:T(256)S(...) while((s32[]{:T(128)}, f32[64,64,256]{2,1,0:T(8,128)}, ...), condition=%wide.region_4.5_spmd, body=%wide.region_2.4_spmd.sunk | while | flops 1613236224 | bytes 69214120 | solution.py:34
  83.2 0.7 add_compare_fusion.4
  83.9 3.1 dynamic-slice_select_fusion.4
  87.0 5.6 %copy.22 = f32[128,64,64]{2,1,0:T(8,128)} copy(f32[128,64,64]{0,2,1:T(8,128)} %bitcast.40) | data formatting | bytes 4194304 | tf_op jit(solution)/shard_map/while/body/eval_jaxpr/reshape | solution.py:30
  92.7 4.3 gather_fusion
  97.0 15.5 %fusion.25 = f32[128,64,256]{2,1,0:T(8,128)} fusion(f32[128,64,64]{2,1,0:T(8,128)} %copy.22, f32[128,64,256]{2,1,0:T(8,128)} %gather_fusion), kind=kOutput, calls=%fused_computation.33.clone.1 | convolution fusion | flops 1610612736 | bytes 18874368 | tf_op jit(solution)/shard_map/while/body/eval_jaxpr/kab,kbf->kaf/dot_general | solution.py:31
  112.5 26.5 %scatter_fusion = f32[64,64,256]{2,1,0:T(8,128)} fusion(f32[64,64,256]{2,1,0:T(8,128)} %get-tuple-element.399, s32[128]{0:T(128)S(1)} %get-tuple-element.376, f32[128,64,256]{2,1,0:T(8,128)} %fusion.25), kind=kCustom, calls=%fused_computation.5.clone.1 | custom fusion | flops 2097152 | bytes 25166336 | tf_op jit(solution)/shard_map/while/body/eval_jaxpr/scatter-add | solution.py:32
  139.6 3.1 dynamic-slice_select_fusion.4
  142.7 5.6 %copy.22 = f32[128,64,64]{2,1,0:T(8,128)} copy(f32[128,64,64]{0,2,1:T(8,128)} %bitcast.40) | data formatting | bytes 4194304 | tf_op jit(solution)/shard_map/while/body/eval_jaxpr/reshape | solution.py:30
  148.4 4.3 gather_fusion
  152.7 15.5 %fusion.25 = f32[128,64,256]{2,1,0:T(8,128)} fusion(f32[128,64,64]{2,1,0:T(8,128)} %copy.22, f32[128,64,256]{2,1,0:T(8,128)} %gather_fusion), kind=kOutput, calls=%fused_computation.33.clone.1 | convolution fusion | flops 1610612736 | bytes 18874368 | tf_op jit(solution)/shard_map/while/body/eval_jaxpr/kab,kbf->kaf/dot_general | solution.py:31
  168.2 26.7 %scatter_fusion = f32[64,64,256]{2,1,0:T(8,128)} fusion(f32[64,64,256]{2,1,0:T(8,128)} %get-tuple-element.399, s32[128]{0:T(128)S(1)} %get-tuple-element.376, f32[128,64,256]{2,1,0:T(8,128)} %fusion.25), kind=kCustom, calls=%fused_computation.5.clone.1 | custom fusion | flops 2097152 | bytes 25166336 | tf_op jit(solution)/shard_map/while/body/eval_jaxpr/scatter-add | solution.py:32
  194.9 73.7 %reduce-scatter.3.cloned.1.call-done = f32[256,256]{1,0:T(8,128)} async-done(((f32[4096,256]{1,0:T(8,128)}), f32[256,256]{1,0:T(8,128)}) %reduce-scatter.3.cloned.1.call-update) | async-done | bytes 262160 | tf_op jit(solution)/shard_map/reduce_scatter | solution.py:93
  268.6 2.1 fusion.2
  270.7 1.1 fusion.5
  272.1 2.3 fusion.6
  274.4 48.1 %all-gather.2.cloned.1.call-done = f32[4096,256]{1,0:T(8,128)} async-done(((f32[256,256]{1,0:T(8,128)}), f32[4096,256]{1,0:T(8,128)}) %all-gather.2.cloned.1.call-update) | async-done | bytes 4194320 | tf_op jit(solution)/shard_map/all_gather | solution.py:99
  322.8 97.1 %while.27 = (s32[]{:T(128)}, f32[32,64,256]{2,1,0:T(8,128)S(1)}, s32[256]{0:T(256)S(1)}, s32[]{:T(128)}, f32[256,4096]{0,1:T(8,128)}, /*index=5*/s32[256]{0:T(25...) while((s32[]{:T(128)}, f32[32,64,256]{2,1,0:T(8,128)S(1)}, ...), condition=%wide.region_8.9_spmd, body=%wide.region_6.8_spmd.sunk | while | flops 1613236224 | bytes 69214120 | solution.py:34
  322.8 0.7 add_compare_fusion.5
  323.4 3.1 dynamic-slice_select_fusion.5
  326.5 5.6 %copy.23 = f32[128,64,64]{1,2,0:T(8,128)} copy(f32[128,64,64]{0,2,1:T(8,128)} %bitcast.41) | data formatting | bytes 4194304 | tf_op jit(solution)/shard_map/while/body/eval_jaxpr/reshape | solution.py:30
  332.2 6.5 %gather_fusion.1 = f32[128,64,256]{2,1,0:T(8,128)} fusion(f32[64,64,256]{2,1,0:T(8,128)} %get-tuple-element.448, s32[1024]{0:T(1024)S(1)} %pad_clamp_fusion.6), kind=kCustom, calls=%fused_computation.1.clone.1 | custom fusion | bytes 16777728 | tf_op jit(solution)/shard_map/while/body/eval_jaxpr/gather | solution.py:31
  338.7 15.5 %fusion.28 = f32[128,64,256]{2,1,0:T(8,128)} fusion(f32[128,64,64]{1,2,0:T(8,128)} %copy.23, f32[128,64,256]{2,1,0:T(8,128)} %gather_fusion.1), kind=kOutput, calls=%fused_computation.34.clone.1 | convolution fusion | flops 1610612736 | bytes 18874368 | tf_op jit(solution)/shard_map/while/body/eval_jaxpr/kba,kbf->kaf/dot_general | solution.py:31
  354.2 17.1 %scatter_fusion.1 = f32[32,64,256]{2,1,0:T(8,128)S(1)} fusion(f32[32,64,256]{2,1,0:T(8,128)S(1)} %get-tuple-element.432, s32[128]{0:T(128)S(1)} %get-tuple-element.385, f32[128,64,256]{2,1,0:T(8,128)} %fusion.28), kind=kCustom, calls=%fused_computation.6.clone.1 | custom fusion | flops 2097152 | bytes 25166336 | tf_op jit(solution)/shard_map/while/body/eval_jaxpr/scatter-add | solution.py:32
  371.3 0.7 add_compare_fusion.5
  372.0 3.1 dynamic-slice_select_fusion.5
  375.1 5.6 %copy.23 = f32[128,64,64]{1,2,0:T(8,128)} copy(f32[128,64,64]{0,2,1:T(8,128)} %bitcast.41) | data formatting | bytes 4194304 | tf_op jit(solution)/shard_map/while/body/eval_jaxpr/reshape | solution.py:30
  380.8 6.5 %gather_fusion.1 = f32[128,64,256]{2,1,0:T(8,128)} fusion(f32[64,64,256]{2,1,0:T(8,128)} %get-tuple-element.448, s32[1024]{0:T(1024)S(1)} %pad_clamp_fusion.6), kind=kCustom, calls=%fused_computation.1.clone.1 | custom fusion | bytes 16777728 | tf_op jit(solution)/shard_map/while/body/eval_jaxpr/gather | solution.py:31
  387.2 15.5 %fusion.28 = f32[128,64,256]{2,1,0:T(8,128)} fusion(f32[128,64,64]{1,2,0:T(8,128)} %copy.23, f32[128,64,256]{2,1,0:T(8,128)} %gather_fusion.1), kind=kOutput, calls=%fused_computation.34.clone.1 | convolution fusion | flops 1610612736 | bytes 18874368 | tf_op jit(solution)/shard_map/while/body/eval_jaxpr/kba,kbf->kaf/dot_general | solution.py:31
  402.7 17.1 %scatter_fusion.1 = f32[32,64,256]{2,1,0:T(8,128)S(1)} fusion(f32[32,64,256]{2,1,0:T(8,128)S(1)} %get-tuple-element.432, s32[128]{0:T(128)S(1)} %get-tuple-element.385, f32[128,64,256]{2,1,0:T(8,128)} %fusion.28), kind=kCustom, calls=%fused_computation.6.clone.1 | custom fusion | flops 2097152 | bytes 25166336 | tf_op jit(solution)/shard_map/while/body/eval_jaxpr/scatter-add | solution.py:32
  419.9 1.3 copy-done.2
  421.2 65.0 %psum.15 = f32[256]{0:T(256)S(1)} all-reduce(f32[256]{0:T(256)S(1)} %get-tuple-element.286), channel_id=1, replica_groups=mesh['row'=16,'col'=8] {'row','col'}, use_global_device_ids=true, to_apply=%region_12.13 | all-reduce | flops 256 | bytes 2048 | tf_op jit(solution)/shard_map/psum | solution.py:117
  486.8 1.7 broadcast_multiply_fusion
  488.5 16.8 %reduce-scatter.5.cloned.1.call-done = f32[256,256]{1,0:T(8,128)} async-done(((f32[2048,256]{1,0:T(8,128)}), f32[256,256]{1,0:T(8,128)}) %reduce-scatter.5.cloned.1.call-update) | async-done | bytes 262160 | tf_op jit(solution)/shard_map/reduce_scatter | solution.py:112
  (44 shorter events, 3.3 us)
Async XLA Ops:
  7.2 261.4 %copy-start = (f32[256,256]{1,0:T(8,128)S(1)}, f32[256,256]{1,0:T(8,128)}, u32[]{:S(2)}) copy-start(f32[256,256]{1,0:T(8,128)} %param.19) | copy-start | bytes 786436
  13.8 20.6 %all-to-all-start.1 = ((f32[128,1,16]{2,1,0:T(1,128)}), f32[128,1,16]{2,1,0:T(1,128)S(1)}, u32[]{:S(2)}, u32[]{:S(2)}) async-start(f32[128,1,16]{2,1,0:T(1,128)} %bitcast.9), calls=%async_computation.1 | async-start | bytes 131072 | tf_op jit(solution)/shard_map/all_to_all | solution.py:74
  36.1 35.1 %all-to-all-start = ((f32[128,16,256]{2,1,0:T(8,128)}), f32[128,16,256]{2,1,0:T(8,128)S(1)}, u32[]{:S(2)}, u32[]{:S(2)}) async-start(f32[128,16,256]{2,1,0:T(8,128)} %bitcast.44), calls=%async_computation | async-start | bytes 4194304 | tf_op jit(solution)/shard_map/all_to_all | solution.py:73
  40.7 227.8 %reduce-scatter.3.cloned.1.call-start = ((), (), s32[]{:S(2)}) async-start(), calls=%async_computation.4 | async-start | bytes 4456448 | tf_op jit(solution)/shard_map/reduce_scatter | solution.py:93
  71.1 1.4 copy-start.3
  80.7 2.5 copy-start.4
  80.7 2.5 copy-start.5
  194.8 73.8 %copy-start.6 = (f32[256,256]{1,0:T(8,128)S(1)}, f32[256,256]{1,0:T(8,128)}, u32[]{:S(2)}) copy-start(f32[256,256]{1,0:T(8,128)} %param.21) | copy-start | bytes 786436
  194.8 73.8 %copy-start.7 = (f32[256]{0:T(256)S(1)}, f32[256]{0:T(256)}, u32[]{:S(2)}) copy-start(f32[256]{0:T(256)} %param.20) | copy-start | bytes 3076
  194.8 127.7 %all-gather.2.cloned.1.call-start = ((), (), s32[]{:S(2)}) async-start(), calls=%async_computation.5 | async-start | bytes 4456448 | tf_op jit(solution)/shard_map/all_gather | solution.py:99
  271.8 215.0 %all-reduce.2.cloned.1.call-start = ((), (), s32[]{:S(2)}) async-start(), calls=%async_computation.7 | async-start | bytes 524288 | tf_op jit(solution)/shard_map/psum | solution.py:117
  274.4 230.9 %reduce-scatter.5.cloned.1.call-start = ((), (), s32[]{:S(2)}) async-start(), calls=%async_computation.6 | async-start | bytes 2359296 | tf_op jit(solution)/shard_map/reduce_scatter | solution.py:112
  419.8 1.4 copy-start.2
  419.8 85.5 %copy-start.1 = (f32[256,256]{1,0:T(8,128)S(1)}, f32[256,256]{1,0:T(8,128)}, u32[]{:S(2)}) copy-start(f32[256,256]{1,0:T(8,128)} %param.19) | copy-start | bytes 786436
Sparse Core Ops, SparseCore 0:
  195.0 73.5 reduce-scatter.2
  272.0 50.5 all-gather.1
  327.9 142.9 all-reduce.1
  473.7 31.5 reduce-scatter.4
where the time goes:
time: 514 us; the launch traced here: 512 us
  waiting for transfers between devices  166 us (32%)
  other arithmetic  114 us (22%)
  local copies, waits for them, and re-layouts  69.6 us (14%)
  matrix products  67.5 us (13%)
  blocking collectives  65 us (13%)
  starting transfers between devices  16.2 us (3%)
  between operations  13.9 us (3%)
    scatter-add x4, other arithmetic, one_group(): return partial_sum.at[into_at].add(terms)  87.3 us
    reduce_scatter x1, waiting for transfers between devices, on_device(): lax.psum_scatter(partial_value, 'row', scatter_dimension=0, tiled=True)  73.7 us
    psum x1, blocking collectives, on_device(): grad_w, grad_b = lax.psum((local_w, local_b), ('row', 'col'))  65 us
    dot_general x4, matrix products, one_group(): jnp.einsum(pattern, group_vals, source_blocks[from_at], precision=precise)  62 us
    all_gather x1, waiting for transfers between devices, on_device(): column = lax.all_gather(grad_hidden, 'row', axis=0, tiled=True)  48.1 us
    reshape x4, local copies, waits for them, and re-layouts, one_group(): group_vals = group_vals.reshape(group_size, block_size, block_size)  22.4 us
    gather x4, local copies, waits for them, and re-layouts, one_group(): source_blocks[from_at]  21.6 us
    all_to_all x1, waiting for transfers between devices, on_device(): lax.all_to_all(sent_rows, ('row', 'col'), split_axis=0, concat_axis=0, ti...  19.4 us
  transfers between devices with their start and end apart: 6, of which 5 were waited for; matrix products, arithmetic and copies ran while one was open for 22% of the time, Pallas kernels for 0%

commit v1 on v0

--- a/solution.py
+++ b/solution.py
@@ -3,6 +3,7 @@
 import jax.numpy as jnp
 from jax import lax
 from jax.sharding import PartitionSpec as P
+from jax.lax import axis_index, ppermute, psum
 
 precise = lax.Precision.HIGHEST
 
@@ -96,7 +97,25 @@
     output = preact * squashed
     grad_pre = cotangent * squashed * (1.0 + preact * (1.0 - squashed))
     grad_hidden = jnp.dot(grad_pre, weight.T, precision=precise)
-    column = lax.all_gather(grad_hidden, "row", axis=0, tiled=True)
+    part_now, high, new = (psum(1, "row"), axis_index("row"), grad_hidden.shape[0])
+    blocks_here = [(w, (w + 1) % part_now) for w in range(part_now)]
+    vals = [(w, (w - 1) % part_now) for w in range(part_now)]
+    column = jnp.zeros(
+        (*grad_hidden.shape[:0], part_now * new, *grad_hidden.shape[1:]), grad_hidden.dtype
+    )
+    column = lax.dynamic_update_slice_in_dim(column, grad_hidden, high * new, axis=0)
+    arr_next = part_now // 2
+    view_out = shaped = grad_hidden
+    for u in range(1, arr_next + 1):
+        view_out = ppermute(view_out, "row", blocks_here)
+        column = lax.dynamic_update_slice_in_dim(
+            column, view_out, (high - u) % part_now * new, axis=0
+        )
+        if u < part_now - arr_next:
+            shaped = ppermute(shaped, "row", vals)
+            column = lax.dynamic_update_slice_in_dim(
+                column, shaped, (high + u) % part_now * new, axis=0
+            )
     partial_x = accumulate(
         jnp.zeros((in_blocks, block_size, feat_width), jnp.float32),
         column.reshape(out_blocks, block_size, feat_width),

time: 514 us -> 538 us (1.047)
  starting transfers between devices: 16.2 us -> 55.2 us
  waiting for transfers between devices: 166 us -> 135 us
  local copies, waits for them, and re-layouts: 69.6 us -> 82.6 us
    all_gather x1 -> x0, waiting for transfers between devices: 48.1 us -> none  [on_device(): column = lax.all_gather(grad_hidden, 'row', axis=0, tiled=True)]
    ppermute x0 -> x15, starting transfers between devices: none -> 39 us  [the longest x7 37.8 us: on_device(): shaped = ppermute(shaped, 'row', vals)]
    ppermute x0 -> x15, waiting for transfers between devices: none -> 34.8 us  [the longest x8 32.8 us: on_device(): view_out = ppermute(view_out, 'row', blocks_here)]
    reduce_scatter x1, waiting for transfers between devices: 16.8 us -> 0.01 us  [on_device(): lax.psum_scatter(partial_x.reshape(group_rows, feat_width), 'col', scatte...]
    dynamic_update_slice x0 -> x15, local copies, waits for them, and re-layouts: none -> 10.8 us  [the longest x8 5.73 us: on_device(): lax.dynamic_update_slice_in_dim(column, view_out, (high - u) % part_now *...]
  transfers between devices with their start and end apart: 6 -> 20, of which waited for: 5 -> 14; matrix products, arithmetic and copies ran while one was open for 22% -> 23% of each run, Pallas kernels for 0% -> 0%
where the time goes in v1:
time: 538 us; the launch traced here: 531 us
  waiting for transfers between devices  135 us (25%)
  other arithmetic  114 us (21%)
  local copies, waits for them, and re-layouts  82.6 us (15%)
  matrix products  66.7 us (12%)
  blocking collectives  62.6 us (12%)
  starting transfers between devices  55.2 us (10%)
  between operations  14.1 us (3%)
    scatter-add x4, other arithmetic, one_group(): return partial_sum.at[into_at].add(terms)  87.3 us
    reduce_scatter x1, waiting for transfers between devices, on_device(): lax.psum_scatter(partial_value, 'row', scatter_dimension=0, tiled=True)  73.4 us
    psum x1, blocking collectives, on_device(): grad_w, grad_b = lax.psum((local_w, local_b), ('row', 'col'))  62.6 us
    dot_general x4, matrix products, one_group(): jnp.einsum(pattern, group_vals, source_blocks[from_at], precision=precise)  62.1 us
    ppermute x7, starting transfers between devices, on_device(): shaped = ppermute(shaped, 'row', vals)  37.8 us
    ppermute x8, waiting for transfers between devices, on_device(): view_out = ppermute(view_out, 'row', blocks_here)  32.8 us
    reshape x4, local copies, waits for them, and re-layouts, one_group(): group_vals = group_vals.reshape(group_size, block_size, block_size)  22.5 us
    gather x4, local copies, waits for them, and re-layouts, one_group(): source_blocks[from_at]  21.6 us
  transfers between devices with their start and end apart: 20, of which 14 were waited for; matrix products, arithmetic and copies ran while one was open for 23% of the time, Pallas kernels for 0%

profile of v1, /device:TPU:0, one launch (start us, length us, event | category | flops | bytes accessed | tf_op | source)
XLA Modules:
  0.0 530.8 jit_solution(737384627845460811)
XLA Ops:
  7.9 3.2 sort.34
  13.8 11.2 %all-to-all-start.1 = ((f32[128,1,16]{2,1,0:T(1,128)}), f32[128,1,16]{2,1,0:T(1,128)S(1)}, u32[]{:S(2)}, u32[]{:S(2)}) async-start(f32[128,1,16]{2,1,0:T(1,128)} %bitcast.9), calls=%async_computation.1 | async-start | bytes 131072 | tf_op jit(solution)/shard_map/all_to_all | solution.py:75
  26.9 7.5 %all-to-all-done.1 = f32[128,1,16]{2,1,0:T(1,128)S(1)} async-done(((f32[128,1,16]{2,1,0:T(1,128)}), f32[128,1,16]{2,1,0:T(1,128)S(1)}, u32[]{:S(2)}, u32[]{:S(2)}) %all-to-all-start.1) | async-done | bytes 8224 | tf_op jit(solution)/shard_map/all_to_all | solution.py:75
  36.1 4.6 all-to-all-start
  40.8 5.6 %copy.19 = f32[1,1,256,4096]{2,3,1,0:T(8,128)} copy(f32[1,1,256,4096]{3,2,1,0:T(8,128)} %param.15) | data formatting | bytes 8388608 | tf_op args[2]
  46.7 5.0 sort.35
  51.7 19.4 %all-to-all-done = f32[128,16,256]{2,1,0:T(8,128)S(1)} async-done(((f32[128,16,256]{2,1,0:T(8,128)}), f32[128,16,256]{2,1,0:T(8,128)S(1)}, u32[]{:S(2)}, u32[]{:S(2)}) %all-to-all-start) | async-done | bytes 2097184 | tf_op jit(solution)/shard_map/all_to_all | solution.py:74
  72.5 8.2 %gather_fusion.4 = f32[2048,256]{1,0:T(8,128)S(1)} fusion(f32[2048,256]{1,0:T(8,128)} %bitcast.41, s32[2048]{0:T(1024)S(1)} %fusion.1), kind=kCustom, calls=%fused_computation.4 | custom fusion | bytes 4202496 | tf_op jit(solution)/shard_map/gather | solution.py:78
  80.7 2.5 broadcast_in_dim.96
  83.2 112.0 %while.26 = (s32[]{:T(128)}, f32[64,64,256]{2,1,0:T(8,128)}, s32[256]{0:T(256)S(1)}, s32[]{:T(128)}, f32[256,4096]{0,1:T(8,128)}, /*index=5*/s32[256]{0:T(256)S(...) while((s32[]{:T(128)}, f32[64,64,256]{2,1,0:T(8,128)}, ...), condition=%wide.region_4.5_spmd, body=%wide.region_2.4_spmd.sunk | while | flops 1613236224 | bytes 69214128 | solution.py:35
  84.4 3.1 dynamic-slice_select_fusion.4
  87.4 5.6 %copy.22 = f32[128,64,64]{2,1,0:T(8,128)} copy(f32[128,64,64]{0,2,1:T(8,128)} %bitcast.39) | data formatting | bytes 4194304 | tf_op jit(solution)/shard_map/while/body/eval_jaxpr/reshape | solution.py:31
  93.0 4.3 gather_fusion
  97.4 15.5 %fusion.24 = f32[128,64,256]{2,1,0:T(8,128)} fusion(f32[128,64,64]{2,1,0:T(8,128)} %copy.22, f32[128,64,256]{2,1,0:T(8,128)} %gather_fusion), kind=kOutput, calls=%fused_computation.49.clone.1 | convolution fusion | flops 1610612736 | bytes 18874368 | tf_op jit(solution)/shard_map/while/body/eval_jaxpr/kab,kbf->kaf/dot_general | solution.py:32
  112.8 26.6 %scatter_fusion = f32[64,64,256]{2,1,0:T(8,128)} fusion(f32[64,64,256]{2,1,0:T(8,128)} %get-tuple-element.401, s32[128]{0:T(128)S(1)} %get-tuple-element.378, f32[128,64,256]{2,1,0:T(8,128)} %fusion.24), kind=kCustom, calls=%fused_computation.5.clone.1 | custom fusion | flops 2097152 | bytes 25166336 | tf_op jit(solution)/shard_map/while/body/eval_jaxpr/scatter-add | solution.py:33
  140.2 3.1 dynamic-slice_select_fusion.4
  143.2 5.6 %copy.22 = f32[128,64,64]{2,1,0:T(8,128)} copy(f32[128,64,64]{0,2,1:T(8,128)} %bitcast.39) | data formatting | bytes 4194304 | tf_op jit(solution)/shard_map/while/body/eval_jaxpr/reshape | solution.py:31
  148.8 4.3 gather_fusion
  153.1 15.5 %fusion.24 = f32[128,64,256]{2,1,0:T(8,128)} fusion(f32[128,64,64]{2,1,0:T(8,128)} %copy.22, f32[128,64,256]{2,1,0:T(8,128)} %gather_fusion), kind=kOutput, calls=%fused_computation.49.clone.1 | convolution fusion | flops 1610612736 | bytes 18874368 | tf_op jit(solution)/shard_map/while/body/eval_jaxpr/kab,kbf->kaf/dot_general | solution.py:32
  168.6 26.6 %scatter_fusion = f32[64,64,256]{2,1,0:T(8,128)} fusion(f32[64,64,256]{2,1,0:T(8,128)} %get-tuple-element.401, s32[128]{0:T(128)S(1)} %get-tuple-element.378, f32[128,64,256]{2,1,0:T(8,128)} %fusion.24), kind=kCustom, calls=%fused_computation.5.clone.1 | custom fusion | flops 2097152 | bytes 25166336 | tf_op jit(solution)/shard_map/while/body/eval_jaxpr/scatter-add | solution.py:33
  195.5 73.4 %reduce-scatter.3.cloned.1.call-done = f32[256,256]{1,0:T(8,128)} async-done(((f32[4096,256]{1,0:T(8,128)}), f32[256,256]{1,0:T(8,128)}) %reduce-scatter.3.cloned.1.call-update) | async-done | bytes 262160 | tf_op jit(solution)/shard_map/reduce_scatter | solution.py:94
  271.1 2.2 broadcast_in_dim.103
  275.5 4.3 collective-permute-start.1
  279.8 4.3 collective-permute-done
  284.1 5.3 %collective-permute-start.3 = (f32[256,256]{1,0:T(8,128)S(1)}, f32[256,256]{1,0:T(8,128)S(1)}, u32[]{:S(2)}, u32[]{:S(2)}) collective-permute-start(f32[256,256]{1,0:T(8,128)S(1)} %collective-permute-done.1), channel_id=1, source_target_pairs={{0,120},{8,0},{16,8},{24,16},{32,24},{40,32},{48,40},{56,48},{64,5... | collective-permute-start | bytes 786440 | tf_op jit(solution)/shard_map/ppermute | solution.py:115
  289.5 4.3 collective-permute-done.2
  293.8 5.3 %collective-permute-start.5 = (f32[256,256]{1,0:T(8,128)S(1)}, f32[256,256]{1,0:T(8,128)S(1)}, u32[]{:S(2)}, u32[]{:S(2)}) collective-permute-start(f32[256,256]{1,0:T(8,128)S(1)} %collective-permute-done.3), channel_id=1, source_target_pairs={{0,120},{8,0},{16,8},{24,16},{32,24},{40,32},{48,40},{56,48},{64,5... | collective-permute-start | bytes 786440 | tf_op jit(solution)/shard_map/ppermute | solution.py:115
  299.2 4.3 collective-permute-done.4
  305.6 5.3 %collective-permute-start.7 = (f32[256,256]{1,0:T(8,128)S(1)}, f32[256,256]{1,0:T(8,128)S(1)}, u32[]{:S(2)}, u32[]{:S(2)}) collective-permute-start(f32[256,256]{1,0:T(8,128)S(1)} %collective-permute-done.5), channel_id=1, source_target_pairs={{0,120},{8,0},{16,8},{24,16},{32,24},{40,32},{48,40},{56,48},{64,5... | collective-permute-start | bytes 786440 | tf_op jit(solution)/shard_map/ppermute | solution.py:115
  315.9 5.8 %collective-permute-start.9 = (f32[256,256]{1,0:T(8,128)S(1)}, f32[256,256]{1,0:T(8,128)S(1)}, u32[]{:S(2)}, u32[]{:S(2)}) collective-permute-start(f32[256,256]{1,0:T(8,128)S(1)} %collective-permute-done.7), channel_id=1, source_target_pairs={{0,120},{8,0},{16,8},{24,16},{32,24},{40,32},{48,40},{56,48},{64,5... | collective-permute-start | bytes 786440 | tf_op jit(solution)/shard_map/ppermute | solution.py:115
  322.4 3.0 collective-permute-done.8
  327.8 5.8 %collective-permute-start.11 = (f32[256,256]{1,0:T(8,128)S(1)}, f32[256,256]{1,0:T(8,128)S(1)}, u32[]{:S(2)}, u32[]{:S(2)}) collective-permute-start(f32[256,256]{1,0:T(8,128)S(1)} %collective-permute-done.9), channel_id=1, source_target_pairs={{0,120},{8,0},{16,8},{24,16},{32,24},{40,32},{48,40},{56,48},{64,5... | collective-permute-start | bytes 786440 | tf_op jit(solution)/shard_map/ppermute | solution.py:115
  334.3 3.7 collective-permute-done.10
  340.0 5.8 %collective-permute-start.13 = (f32[256,256]{1,0:T(8,128)S(1)}, f32[256,256]{1,0:T(8,128)S(1)}, u32[]{:S(2)}, u32[]{:S(2)}) collective-permute-start(f32[256,256]{1,0:T(8,128)S(1)} %collective-permute-done.11), channel_id=1, source_target_pairs={{0,120},{8,0},{16,8},{24,16},{32,24},{40,32},{48,40},{56,48},{64,5... | collective-permute-start | bytes 786440 | tf_op jit(solution)/shard_map/ppermute | solution.py:115
  346.5 3.3 collective-permute-done.12
  352.2 7.6 %collective-permute-done.14 = f32[256,256]{1,0:T(8,128)S(1)} collective-permute-done((f32[256,256]{1,0:T(8,128)S(1)}, f32[256,256]{1,0:T(8,128)S(1)}, u32[]{:S(2)}, u32[]{:S(2)}) %collective-permute-start.14) | collective-permute-done | bytes 262176 | tf_op jit(solution)/shard_map/ppermute | solution.py:110
  360.7 97.2 %while.27 = (s32[]{:T(128)}, f32[32,64,256]{2,1,0:T(8,128)S(1)}, s32[256]{0:T(256)S(1)}, s32[]{:T(128)}, f32[256,4096]{0,1:T(8,128)}, /*index=5*/s32[256]{0:T(25...) while((s32[]{:T(128)}, f32[32,64,256]{2,1,0:T(8,128)S(1)}, ...), condition=%wide.region_8.9_spmd, body=%wide.region_6.8_spmd.sunk | while | flops 1613236224 | bytes 69214128 | solution.py:35
  361.5 3.1 dynamic-slice_select_fusion.5
  364.5 5.6 %copy.23 = f32[128,64,64]{1,2,0:T(8,128)} copy(f32[128,64,64]{0,2,1:T(8,128)} %bitcast.40) | data formatting | bytes 4194304 | tf_op jit(solution)/shard_map/while/body/eval_jaxpr/reshape | solution.py:31
  370.2 6.5 %gather_fusion.1 = f32[128,64,256]{2,1,0:T(8,128)} fusion(f32[64,64,256]{2,1,0:T(8,128)} %get-tuple-element.450, s32[1024]{0:T(1024)S(1)} %pad_clamp_fusion.6), kind=kCustom, calls=%fused_computation.1.clone.1 | custom fusion | bytes 16777728 | tf_op jit(solution)/shard_map/while/body/eval_jaxpr/gather | solution.py:32
  376.7 15.5 %fusion.27 = f32[128,64,256]{2,1,0:T(8,128)} fusion(f32[128,64,64]{1,2,0:T(8,128)} %copy.23, f32[128,64,256]{2,1,0:T(8,128)} %gather_fusion.1), kind=kOutput, calls=%fused_computation.50.clone.1 | convolution fusion | flops 1610612736 | bytes 18874368 | tf_op jit(solution)/shard_map/while/body/eval_jaxpr/kba,kbf->kaf/dot_general | solution.py:32
  392.2 17.1 %scatter_fusion.1 = f32[32,64,256]{2,1,0:T(8,128)S(1)} fusion(f32[32,64,256]{2,1,0:T(8,128)S(1)} %get-tuple-element.434, s32[128]{0:T(128)S(1)} %get-tuple-element.387, f32[128,64,256]{2,1,0:T(8,128)} %fusion.27), kind=kCustom, calls=%fused_computation.6.clone.1 | custom fusion | flops 2097152 | bytes 25166336 | tf_op jit(solution)/shard_map/while/body/eval_jaxpr/scatter-add | solution.py:33
  410.0 3.1 dynamic-slice_select_fusion.5
  413.1 5.6 %copy.23 = f32[128,64,64]{1,2,0:T(8,128)} copy(f32[128,64,64]{0,2,1:T(8,128)} %bitcast.40) | data formatting | bytes 4194304 | tf_op jit(solution)/shard_map/while/body/eval_jaxpr/reshape | solution.py:31
  418.7 6.5 %gather_fusion.1 = f32[128,64,256]{2,1,0:T(8,128)} fusion(f32[64,64,256]{2,1,0:T(8,128)} %get-tuple-element.450, s32[1024]{0:T(1024)S(1)} %pad_clamp_fusion.6), kind=kCustom, calls=%fused_computation.1.clone.1 | custom fusion | bytes 16777728 | tf_op jit(solution)/shard_map/while/body/eval_jaxpr/gather | solution.py:32
  425.2 15.6 %fusion.27 = f32[128,64,256]{2,1,0:T(8,128)} fusion(f32[128,64,64]{1,2,0:T(8,128)} %copy.23, f32[128,64,256]{2,1,0:T(8,128)} %gather_fusion.1), kind=kOutput, calls=%fused_computation.50.clone.1 | convolution fusion | flops 1610612736 | bytes 18874368 | tf_op jit(solution)/shard_map/while/body/eval_jaxpr/kba,kbf->kaf/dot_general | solution.py:32
  440.8 17.1 %scatter_fusion.1 = f32[32,64,256]{2,1,0:T(8,128)S(1)} fusion(f32[32,64,256]{2,1,0:T(8,128)S(1)} %get-tuple-element.434, s32[128]{0:T(128)S(1)} %get-tuple-element.387, f32[128,64,256]{2,1,0:T(8,128)} %fusion.27), kind=kCustom, calls=%fused_computation.6.clone.1 | custom fusion | flops 2097152 | bytes 25166336 | tf_op jit(solution)/shard_map/while/body/eval_jaxpr/scatter-add | solution.py:33
  459.2 62.6 %psum.15 = f32[256]{0:T(256)S(1)} all-reduce(f32[256]{0:T(256)S(1)} %get-tuple-element.286), channel_id=1, replica_groups=mesh['row'=16,'col'=8] {'row','col'}, use_global_device_ids=true, to_apply=%region_12.13 | all-reduce | flops 256 | bytes 2048 | tf_op jit(solution)/shard_map/psum | solution.py:136
  (89 shorter events, 36.5 us)
Async XLA Ops:
  7.2 261.7 %copy-start = (f32[256,256]{1,0:T(8,128)S(1)}, f32[256,256]{1,0:T(8,128)}, u32[]{:S(2)}) copy-start(f32[256,256]{1,0:T(8,128)} %param.19) | copy-start | bytes 786436
  13.8 20.6 %all-to-all-start.1 = ((f32[128,1,16]{2,1,0:T(1,128)}), f32[128,1,16]{2,1,0:T(1,128)S(1)}, u32[]{:S(2)}, u32[]{:S(2)}) async-start(f32[128,1,16]{2,1,0:T(1,128)} %bitcast.9), calls=%async_computation.1 | async-start | bytes 131072 | tf_op jit(solution)/shard_map/all_to_all | solution.py:75
  36.1 35.1 %all-to-all-start = ((f32[128,16,256]{2,1,0:T(8,128)}), f32[128,16,256]{2,1,0:T(8,128)S(1)}, u32[]{:S(2)}, u32[]{:S(2)}) async-start(f32[128,16,256]{2,1,0:T(8,128)} %bitcast.43), calls=%async_computation | async-start | bytes 4194304 | tf_op jit(solution)/shard_map/all_to_all | solution.py:74
  40.7 228.2 %reduce-scatter.3.cloned.1.call-start = ((), (), s32[]{:S(2)}) async-start(), calls=%async_computation.4 | async-start | bytes 4456448 | tf_op jit(solution)/shard_map/reduce_scatter | solution.py:94
  71.1 1.3 copy-start.3
  80.7 2.5 copy-start.5
  80.7 2.5 copy-start.6
  195.2 73.7 %copy-start.7 = (f32[256,256]{1,0:T(8,128)S(1)}, f32[256,256]{1,0:T(8,128)}, u32[]{:S(2)}) copy-start(f32[256,256]{1,0:T(8,128)} %param.21) | copy-start | bytes 786436
  195.2 73.7 %copy-start.8 = (f32[256]{0:T(256)S(1)}, f32[256]{0:T(256)}, u32[]{:S(2)}) copy-start(f32[256]{0:T(256)} %param.20) | copy-start | bytes 3076
  195.2 327.2 %all-reduce.2.cloned.1.call-start = ((), (), s32[]{:S(2)}) async-start(), calls=%async_computation.6 | async-start | bytes 524288 | tf_op jit(solution)/shard_map/psum | solution.py:136
  268.9 34.6 %copy-start.4 = (f32[256,256]{1,0:T(8,128)S(1)}, f32[256,256]{1,0:T(8,128)}, u32[]{:S(2)}) copy-start(f32[256,256]{1,0:T(8,128)} %reduce-scatter.3.cloned.1.call-done) | copy-start | bytes 786436
  274.4 9.7 %collective-permute-start = (f32[256,256]{1,0:T(8,128)S(1)}, f32[256,256]{1,0:T(8,128)S(1)}, u32[]{:S(2)}, u32[]{:S(2)}) collective-permute-start(f32[256,256]{1,0:T(8,128)S(1)} %get-tuple-element.294), channel_id=1, source_target_pairs={{0,8},{8,16},{16,24},{24,32},{32,40},{40,48},{48,56},{56,64},{64,7... | collective-permute-start | bytes 786440 | tf_op jit(solution)/shard_map/ppermute | solution.py:110
  275.5 8.6 %collective-permute-start.1 = (f32[256,256]{1,0:T(8,128)S(1)}, f32[256,256]{1,0:T(8,128)S(1)}, u32[]{:S(2)}, u32[]{:S(2)}) collective-permute-start(f32[256,256]{1,0:T(8,128)S(1)} %get-tuple-element.294), channel_id=1, source_target_pairs={{0,120},{8,0},{16,8},{24,16},{32,24},{40,32},{48,40},{56,48},{64,5... | collective-permute-start | bytes 786440 | tf_op jit(solution)/shard_map/ppermute | solution.py:115
  284.1 9.7 %collective-permute-start.2 = (f32[256,256]{1,0:T(8,128)S(1)}, f32[256,256]{1,0:T(8,128)S(1)}, u32[]{:S(2)}, u32[]{:S(2)}) collective-permute-start(f32[256,256]{1,0:T(8,128)S(1)} %collective-permute-done), channel_id=1, source_target_pairs={{0,8},{8,16},{16,24},{24,32},{32,40},{40,48},{48,56},{56,64},{64,7... | collective-permute-start | bytes 786440 | tf_op jit(solution)/shard_map/ppermute | solution.py:110
  284.1 9.7 %collective-permute-start.3 = (f32[256,256]{1,0:T(8,128)S(1)}, f32[256,256]{1,0:T(8,128)S(1)}, u32[]{:S(2)}, u32[]{:S(2)}) collective-permute-start(f32[256,256]{1,0:T(8,128)S(1)} %collective-permute-done.1), channel_id=1, source_target_pairs={{0,120},{8,0},{16,8},{24,16},{32,24},{40,32},{48,40},{56,48},{64,5... | collective-permute-start | bytes 786440 | tf_op jit(solution)/shard_map/ppermute | solution.py:115
  293.8 9.7 %collective-permute-start.4 = (f32[256,256]{1,0:T(8,128)S(1)}, f32[256,256]{1,0:T(8,128)S(1)}, u32[]{:S(2)}, u32[]{:S(2)}) collective-permute-start(f32[256,256]{1,0:T(8,128)S(1)} %collective-permute-done.2), channel_id=1, source_target_pairs={{0,8},{8,16},{16,24},{24,32},{32,40},{40,48},{48,56},{56,64},{64,7... | collective-permute-start | bytes 786440 | tf_op jit(solution)/shard_map/ppermute | solution.py:110
  293.8 11.8 %collective-permute-start.5 = (f32[256,256]{1,0:T(8,128)S(1)}, f32[256,256]{1,0:T(8,128)S(1)}, u32[]{:S(2)}, u32[]{:S(2)}) collective-permute-start(f32[256,256]{1,0:T(8,128)S(1)} %collective-permute-done.3), channel_id=1, source_target_pairs={{0,120},{8,0},{16,8},{24,16},{32,24},{40,32},{48,40},{56,48},{64,5... | collective-permute-start | bytes 786440 | tf_op jit(solution)/shard_map/ppermute | solution.py:115
  303.5 10.3 %collective-permute-start.6 = (f32[256,256]{1,0:T(8,128)S(1)}, f32[256,256]{1,0:T(8,128)S(1)}, u32[]{:S(2)}, u32[]{:S(2)}) collective-permute-start(f32[256,256]{1,0:T(8,128)S(1)} %collective-permute-done.4), channel_id=1, source_target_pairs={{0,8},{8,16},{16,24},{24,32},{32,40},{40,48},{48,56},{56,64},{64,7... | collective-permute-start | bytes 786440 | tf_op jit(solution)/shard_map/ppermute | solution.py:110
  304.9 219.2 %reduce-scatter.5.cloned.1.call-start = ((), (), s32[]{:S(2)}) async-start(), calls=%async_computation.5 | async-start | bytes 2359296 | tf_op jit(solution)/shard_map/reduce_scatter | solution.py:131
  305.6 10.2 %collective-permute-start.7 = (f32[256,256]{1,0:T(8,128)S(1)}, f32[256,256]{1,0:T(8,128)S(1)}, u32[]{:S(2)}, u32[]{:S(2)}) collective-permute-start(f32[256,256]{1,0:T(8,128)S(1)} %collective-permute-done.5), channel_id=1, source_target_pairs={{0,120},{8,0},{16,8},{24,16},{32,24},{40,32},{48,40},{56,48},{64,5... | collective-permute-start | bytes 786440 | tf_op jit(solution)/shard_map/ppermute | solution.py:115
  313.9 11.6 %collective-permute-start.8 = (f32[256,256]{1,0:T(8,128)S(1)}, f32[256,256]{1,0:T(8,128)S(1)}, u32[]{:S(2)}, u32[]{:S(2)}) collective-permute-start(f32[256,256]{1,0:T(8,128)S(1)} %collective-permute-done.6), channel_id=1, source_target_pairs={{0,8},{8,16},{16,24},{24,32},{32,40},{40,48},{48,56},{56,64},{64,7... | collective-permute-start | bytes 786440 | tf_op jit(solution)/shard_map/ppermute | solution.py:110
  315.9 11.9 %collective-permute-start.9 = (f32[256,256]{1,0:T(8,128)S(1)}, f32[256,256]{1,0:T(8,128)S(1)}, u32[]{:S(2)}, u32[]{:S(2)}) collective-permute-start(f32[256,256]{1,0:T(8,128)S(1)} %collective-permute-done.7), channel_id=1, source_target_pairs={{0,120},{8,0},{16,8},{24,16},{32,24},{40,32},{48,40},{56,48},{64,5... | collective-permute-start | bytes 786440 | tf_op jit(solution)/shard_map/ppermute | solution.py:115
  325.5 12.6 %collective-permute-start.10 = (f32[256,256]{1,0:T(8,128)S(1)}, f32[256,256]{1,0:T(8,128)S(1)}, u32[]{:S(2)}, u32[]{:S(2)}) collective-permute-start(f32[256,256]{1,0:T(8,128)S(1)} %collective-permute-done.8), channel_id=1, source_target_pairs={{0,8},{8,16},{16,24},{24,32},{32,40},{40,48},{48,56},{56,64},{64,7... | collective-permute-start | bytes 786440 | tf_op jit(solution)/shard_map/ppermute | solution.py:110
  327.8 12.2 %collective-permute-start.11 = (f32[256,256]{1,0:T(8,128)S(1)}, f32[256,256]{1,0:T(8,128)S(1)}, u32[]{:S(2)}, u32[]{:S(2)}) collective-permute-start(f32[256,256]{1,0:T(8,128)S(1)} %collective-permute-done.9), channel_id=1, source_target_pairs={{0,120},{8,0},{16,8},{24,16},{32,24},{40,32},{48,40},{56,48},{64,5... | collective-permute-start | bytes 786440 | tf_op jit(solution)/shard_map/ppermute | solution.py:115
  338.0 11.7 %collective-permute-start.12 = (f32[256,256]{1,0:T(8,128)S(1)}, f32[256,256]{1,0:T(8,128)S(1)}, u32[]{:S(2)}, u32[]{:S(2)}) collective-permute-start(f32[256,256]{1,0:T(8,128)S(1)} %collective-permute-done.10), channel_id=1, source_target_pairs={{0,8},{8,16},{16,24},{24,32},{32,40},{40,48},{48,56},{56,64},{64,7... | collective-permute-start | bytes 786440 | tf_op jit(solution)/shard_map/ppermute | solution.py:110
  340.0 11.5 %collective-permute-start.13 = (f32[256,256]{1,0:T(8,128)S(1)}, f32[256,256]{1,0:T(8,128)S(1)}, u32[]{:S(2)}, u32[]{:S(2)}) collective-permute-start(f32[256,256]{1,0:T(8,128)S(1)} %collective-permute-done.11), channel_id=1, source_target_pairs={{0,120},{8,0},{16,8},{24,16},{32,24},{40,32},{48,40},{56,48},{64,5... | collective-permute-start | bytes 786440 | tf_op jit(solution)/shard_map/ppermute | solution.py:115
  349.8 10.0 %collective-permute-start.14 = (f32[256,256]{1,0:T(8,128)S(1)}, f32[256,256]{1,0:T(8,128)S(1)}, u32[]{:S(2)}, u32[]{:S(2)}) collective-permute-start(f32[256,256]{1,0:T(8,128)S(1)} %collective-permute-done.12), channel_id=1, source_target_pairs={{0,8},{8,16},{16,24},{24,32},{32,40},{40,48},{48,56},{56,64},{64,7... | collective-permute-start | bytes 786440 | tf_op jit(solution)/shard_map/ppermute | solution.py:110
  457.9 1.3 copy-start.2
  457.9 66.2 %copy-start.1 = (f32[256,256]{1,0:T(8,128)S(1)}, f32[256,256]{1,0:T(8,128)}, u32[]{:S(2)}) copy-start(f32[256,256]{1,0:T(8,128)} %param.19) | copy-start | bytes 786436
Sparse Core Ops, SparseCore 0:
  195.4 73.4 reduce-scatter.2
  305.0 145.7 all-reduce.1
  459.4 30.5 reduce-scatter.4
